TPU v7x, 32 devices: a whole 2x2x4 slice. The times are simulated.
32 devices in a mesh: dp: 8 (over z, y), expert: 4 (over x, core).
Axes of the slice: x: 2, y: 2, z: 4, core: 2. Of those that a mesh axis runs over, the one named last changes fastest.
Arguments:
- tokens: bfloat16 [4096, 1024], P(('dp', 'expert')), may hold values from -6 to 6
- cotangent: bfloat16 [4096, 1024], P(('dp', 'expert')), may hold values from -6 to 6
- expert_ids: int32 [4096, 2], P(('dp', 'expert')), may hold values from 0 to 3, all different within a row; in each aligned block of 128 rows (0 to 127, 128 to 255, ...) at most 128 rows name the same one
- gate_weights: float32 [4096, 2], P(('dp', 'expert')), may hold values from 0.05 to 1
- w_gate: bfloat16 [4, 384, 1024], P('expert'), may hold values from -0.1875 to 0.1875
- w_up: bfloat16 [4, 384, 1024], P('expert'), may hold values from -0.1875 to 0.1875
- w_down: bfloat16 [4, 384, 1024], P('expert'), may hold values from -0.3125 to 0.3125
Outputs:
- layer_out: bfloat16 [4096, 1024], P(('dp', 'expert'))
- grad_tokens: bfloat16 [4096, 1024], P(('dp', 'expert'))
- grad_up: float32 [4, 384, 1024], P('expert', 'dp')
- grad_down: float32 [4, 384, 1024], P('expert', 'dp')
Inputs may be any that keep to these rules, and one draw needn't show every extreme that they name: `expert_ids`: each row names 2 different experts. Among the 128 rows of one device no expert is named more than 128 times, and in every draw some expert is named exactly 128 times by the rows of some device.
All inputs are finite; a program needn't handle non-finite values.
Results may differ from a plain program's by a relative error of at most 0.0065.
Values may be sent and summed in bfloat16 or wider, within the bound.
A program may use at most 64 MiB of HBM per device.

v0:
```python
import jax
import jax.numpy as jnp
from jax import lax
from jax.sharding import PartitionSpec as P


def batched(left_op, right_op, left_dim, right_dim):
    return lax.dot_general(
        left_op,
        right_op,
        (((left_dim,), (right_dim,)), ((0,), (0,))),
        preferred_element_type=jnp.float32,
    )


def forward(received, w_gate, w_up, w_down):
    gate_pre = batched(received, w_gate, 2, 2)
    up_pre = batched(received, w_up, 2, 2)
    gate_sig = jax.nn.sigmoid(gate_pre)
    hidden = (gate_pre * gate_sig * up_pre).astype(jnp.bfloat16)
    expert_out = batched(hidden, w_down, 2, 1).astype(jnp.bfloat16)
    return ((gate_pre, up_pre, gate_sig, hidden), expert_out)


def backward(received, grad_out, saved_acts, w_gate, w_up, w_down):
    gate_pre, up_pre, gate_sig, hidden = saved_acts
    grad_lower = lax.psum_scatter(
        batched(hidden, grad_out, 1, 1), "dp", scatter_dimension=1, tiled=True
    )
    grad_hidden = batched(grad_out, w_down, 2, 2)
    grad_up_pre = (grad_hidden * gate_pre * gate_sig).astype(jnp.bfloat16)
    grad_gate_pre = (grad_hidden * up_pre * gate_sig * (1.0 + gate_pre * (1.0 - gate_sig))).astype(
        jnp.bfloat16
    )
    grad_input = (batched(grad_gate_pre, w_gate, 2, 1) + batched(grad_up_pre, w_up, 2, 1)).astype(
        jnp.bfloat16
    )
    grad_upper = batched(grad_up_pre, received, 1, 1)
    grad_upper = lax.psum_scatter(grad_upper, "dp", scatter_dimension=1, tiled=True)
    return (grad_input, (grad_upper, grad_lower))


def shards(tokens, cotangent, expert_ids, gate_weights, w_gate, w_up, w_down):
    tok_rows, model_width = tokens.shape
    top_count = expert_ids.shape[1]
    local_experts = w_gate.shape[0]
    groups = lax.axis_size("expert")
    experts = local_experts * groups
    capacity = 2 * tok_rows * top_count // experts
    pair_count = tok_rows * top_count
    slot_count = experts * capacity
    flat_ids = expert_ids.reshape(-1)
    flat_gates = gate_weights.reshape(-1)
    onehot = (flat_ids[:, None] == jnp.arange(experts, dtype=jnp.int32)[None, :]).astype(jnp.int32)
    before = jnp.cumsum(onehot, axis=0) - onehot
    slot_rank = jnp.sum(before * onehot, axis=1)
    position = flat_ids * capacity + slot_rank
    matches = position[None, :] == jnp.arange(slot_count, dtype=jnp.int32)[:, None]
    source = (
        jnp.sum(jnp.where(matches, jnp.arange(pair_count, dtype=jnp.int32)[None, :] + 1, 0), axis=1)
        - 1
    )
    filled = source >= 0
    clipped = jnp.maximum(source, 0)
    token_rows = clipped // top_count
    slot_gates = jnp.where(filled, flat_gates[clipped], 0.0)
    sent_tokens = jnp.where(filled[:, None], tokens[token_rows], jnp.zeros((), jnp.bfloat16))
    sent_tokens = sent_tokens.reshape(experts, capacity, model_width)
    sent_grads = (slot_gates[:, None] * cotangent[token_rows].astype(jnp.float32)).astype(
        jnp.bfloat16
    )
    sent_grads = sent_grads.reshape(experts, capacity, model_width)
    received = lax.all_to_all(sent_tokens, "expert", split_axis=0, concat_axis=1, tiled=True)
    saved_acts, expert_out = forward(received, w_gate, w_up, w_down)
    back_out = lax.all_to_all(expert_out, "expert", split_axis=1, concat_axis=0, tiled=True)
    grad_out = lax.all_to_all(sent_grads, "expert", split_axis=0, concat_axis=1, tiled=True)
    grad_input, grads = backward(received, grad_out, saved_acts, w_gate, w_up, w_down)
    back_grad = lax.all_to_all(grad_input, "expert", split_axis=1, concat_axis=0, tiled=True)
    out_rows = (
        back_out.reshape(slot_count, model_width)[position].astype(jnp.float32)
        * flat_gates[:, None]
    )
    layer_out = jnp.sum(out_rows.reshape(tok_rows, top_count, model_width), axis=1).astype(
        jnp.bfloat16
    )
    grad_rows = back_grad.reshape(slot_count, model_width)[position].astype(jnp.float32)
    grad_tokens = jnp.sum(grad_rows.reshape(tok_rows, top_count, model_width), axis=1).astype(
        jnp.bfloat16
    )
    grad_scale = (tok_rows * lax.axis_size("dp") * groups * top_count / experts) ** (-0.5)
    return (layer_out, grad_tokens, grads[0] * grad_scale, grads[1] * grad_scale)


def solution(mesh):
    in_specs = (
        P(("dp", "expert"), None),
        P(("dp", "expert"), None),
        P(("dp", "expert"), None),
        P(("dp", "expert"), None),
        P("expert", None, None),
        P("expert", None, None),
        P("expert", None, None),
    )
    out_specs = (
        P(("dp", "expert"), None),
        P(("dp", "expert"), None),
        P("expert", "dp", None),
        P("expert", "dp", None),
    )
    return jax.shard_map(shards, mesh=mesh, in_specs=in_specs, out_specs=out_specs, check_vma=False)
```

profile of v0, /device:TPU:0, one launch (start us, length us, event | category | flops | bytes accessed | tf_op | source)
XLA Modules:
  0.0 203.4 jit_solution(15513453985991420824)
XLA Ops:
  7.2 0.9 copy.39
  8.4 1.2 reduce-window.6
  10.0 0.2 select_reduce_fusion
  10.2 0.8 copy.45
  11.1 3.5 %gather_fusion.2 = f32[512]{0:T(512)S(1)} fusion(f32[256]{0:T(256)S(1)} %reshape.257, s32[1024]{0:T(1024)S(1)} %pad_clamp_fusion), kind=kCustom, calls=%fused_computation.2 | custom fusion | bytes 6144 | tf_op jit(solution)/shard_map/gather | solution.py:66
  14.7 2.1 %gather_fusion = bf16[512,1024]{1,0:T(8,128)(2,1)S(1)} fusion(bf16[128,1024]{1,0:T(8,128)(2,1)S(1)} %copy-done.1, s32[1024]{0:T(1024)S(1)} %pad_clamp_fusion.2), kind=kCustom, calls=%fused_computation | custom fusion | bytes 2099200 | tf_op jit(solution)/shard_map/gather | solution.py:67
  16.8 1.2 broadcast_select_fusion
  18.0 4.2 %all-to-all-start = ((bf16[4,128,1024]{2,1,0:T(8,128)(2,1)}), bf16[4,128,1024]{2,1,0:T(8,128)(2,1)S(1)}, u32[]{:S(2)}, u32[]{:S(2)}) async-start(bf16[4,128,1024]{2,1,0:T(8,128)(2,1)} %broadcast_select_fusion), calls=%async_computation | async-start | bytes 2097152 | tf_op jit(solution)/shard_map/all_to_all | solution.py:73
  22.2 2.0 %gather_fusion.3 = bf16[512,1024]{1,0:T(8,128)(2,1)S(1)} fusion(bf16[128,1024]{1,0:T(8,128)(2,1)S(1)} %copy-done.2, s32[1024]{0:T(1024)S(1)} %pad_clamp_fusion.2), kind=kCustom, calls=%fused_computation.3 | custom fusion | bytes 2099200 | tf_op jit(solution)/shard_map/gather | solution.py:69
  24.3 1.2 fusion
  25.5 11.1 %all-to-all-done = bf16[4,128,1024]{2,1,0:T(8,128)(2,1)S(1)} async-done(((bf16[4,128,1024]{2,1,0:T(8,128)(2,1)}), bf16[4,128,1024]{2,1,0:T(8,128)(2,1)S(1)}, u32[]{:S(2)}, u32[]{:S(2)}) %all-to-all-start) | async-done | bytes 1048608 | tf_op jit(solution)/shard_map/all_to_all | solution.py:73
  36.6 3.5 %all-to-all-start.2 = ((bf16[4,128,1024]{2,1,0:T(8,128)(2,1)}), bf16[4,128,1024]{2,1,0:T(8,128)(2,1)S(1)}, u32[]{:S(2)}, u32[]{:S(2)}) async-start(bf16[4,128,1024]{2,1,0:T(8,128)(2,1)} %fusion), calls=%async_computation.2 | async-start | bytes 2097152 | tf_op jit(solution)/shard_map/all_to_all | solution.py:76
  40.2 2.9 %fusion.11 = f32[512,384]{1,0:T(8,128)} fusion(bf16[512,1024]{1,0:T(8,128)(2,1)S(1)} %bitcast.83, bf16[1,384,1024]{2,1,0:T(8,128)(2,1)} %param.11), kind=kOutput, calls=%fused_computation.25 | convolution fusion | flops 402653184 | bytes 2621440 | tf_op jit(solution)/shard_map/dot_general | solution.py:8
  43.1 1.6 fusion.7
  44.7 9.8 %all-to-all-done.2 = bf16[4,128,1024]{2,1,0:T(8,128)(2,1)S(1)} async-done(((bf16[4,128,1024]{2,1,0:T(8,128)(2,1)}), bf16[4,128,1024]{2,1,0:T(8,128)(2,1)S(1)}, u32[]{:S(2)}, u32[]{:S(2)}) %all-to-all-start.2) | async-done | bytes 1048608 | tf_op jit(solution)/shard_map/all_to_all | solution.py:76
  54.5 3.0 %multiply_convert_fusion = (bf16[512,384]{1,0:T(8,128)(2,1)S(1)}, bf16[512,384]{1,0:T(8,128)(2,1)S(1)}, f32[512,384]{1,0:T(8,128)}) fusion(f32[512,384]{1,0:T(8,128)} %fusion.11, f32[512,384]{1,0:T(8,128)} %fusion.7, bf16[512,1024]{1,0:T(8,128)(2,1)S(1)} %bitcast.92, bf16[1,384,1024]{2,1,0:T(8,128)(2,1)S(1)} %copy-done), kind=kOutput, calls=%fused_computation.27 | convolution fusion | flops 404422656 | bytes 4980736 | tf_op jit(solution)/shard_map/dot_general | solution.py:8
  57.5 0.8 copy-done.5
  58.3 1.8 convolution_bitcast_fusion
  60.1 0.2 reduce-scatter.3.cloned.1.call-start
  60.4 1.7 convolution_bitcast_fusion.1
  62.1 2.6 %fusion.9 = f32[512,1024]{1,0:T(8,128)S(1)} fusion(bf16[1,384,1024]{2,1,0:T(8,128)(2,1)S(1)} %copy-done.7, f32[512,384]{1,0:T(8,128)} %fusion.11, f32[512,384]{1,0:T(8,128)} %get-tuple-element.10, f32[512,384]{1,0:T(8,128)} %fusion.7), kind=kOutput, calls=%fused_computation.23 | convolution fusion | flops 404619264 | bytes 5242880 | tf_op jit(solution)/shard_map/dot_general | solution.py:8
  64.7 0.7 fusion.2
  65.4 1.6 copy.58
  67.1 0.5 broadcast.255
  67.6 7.8 %reduce.2 = bf16[512,1024]{1,0:T(8,128)(2,1)} reduce(bf16[512,1,1024]{2,1,0:T(2,128)(2,1)S(1)} %bitcast.88, bf16[]{:T(256)} %broadcast.255), dimensions={1}, to_apply=%bitcast.79.reduce_sub_computation | reduce | bytes 2097154
  75.4 3.8 %reshape.318 = bf16[4,2,65536]{2,1,0:T(2,128)(2,1)} reshape(bf16[512,1024]{1,0:T(8,128)(2,1)} %reduce.2) | data formatting | bytes 2097152
  79.2 4.5 %all-to-all-start.3 = ((bf16[4,2,65536]{2,1,0:T(2,128)(2,1)}), bf16[4,2,65536]{2,1,0:T(2,128)(2,1)}, u32[]{:S(2)}, u32[]{:S(2)}) async-start(bf16[4,2,65536]{2,1,0:T(2,128)(2,1)} %reshape.318), calls=%async_computation.3 | async-start | bytes 2097152 | tf_op jit(solution)/shard_map/all_to_all | solution.py:78
  83.7 0.7 fusion.1
  84.4 1.6 copy.59
  86.0 7.8 %reduce.1 = bf16[512,1024]{1,0:T(8,128)(2,1)} reduce(bf16[512,1,1024]{2,1,0:T(2,128)(2,1)S(1)} %bitcast.89, bf16[]{:T(256)} %broadcast.255), dimensions={1}, to_apply=%bitcast.80.reduce_sub_computation | reduce | bytes 2097154
  93.8 3.7 %reshape.316 = bf16[4,2,65536]{2,1,0:T(2,128)(2,1)} reshape(bf16[512,1024]{1,0:T(8,128)(2,1)} %reduce.1) | data formatting | bytes 2097152
  97.6 0.3 all-to-all-done.3
  97.9 3.8 %all-to-all-start.1 = ((bf16[4,2,65536]{2,1,0:T(2,128)(2,1)}), bf16[4,2,65536]{2,1,0:T(2,128)(2,1)S(1)}, u32[]{:S(2)}, u32[]{:S(2)}) async-start(bf16[4,2,65536]{2,1,0:T(2,128)(2,1)} %reshape.316), calls=%async_computation.1 | async-start | bytes 2097152 | tf_op jit(solution)/shard_map/all_to_all | solution.py:75
  102.0 4.0 %reshape.319 = bf16[512,1,1024]{2,1,0:T(2,128)(2,1)} reshape(bf16[4,2,65536]{2,1,0:T(2,128)(2,1)} %all-to-all-done.3) | data formatting | bytes 2097152
  106.0 2.0 copy.56
  108.0 1.2 gather_fusion.4
  109.1 0.2 gather.28
  109.4 6.5 %all-to-all-done.1 = bf16[4,2,65536]{2,1,0:T(2,128)(2,1)S(1)} async-done(((bf16[4,2,65536]{2,1,0:T(2,128)(2,1)}), bf16[4,2,65536]{2,1,0:T(2,128)(2,1)S(1)}, u32[]{:S(2)}, u32[]{:S(2)}) %all-to-all-start.1) | async-done | bytes 1048608 | tf_op jit(solution)/shard_map/all_to_all | solution.py:75
  115.9 2.3 %reshape.317 = bf16[512,1,1024]{2,1,0:T(2,128)(2,1)} reshape(bf16[4,2,65536]{2,1,0:T(2,128)(2,1)S(1)} %all-to-all-done.1) | data formatting | bytes 2097152
  118.2 2.0 copy.57
  120.2 1.2 gather_fusion.1
  121.3 0.7 reshape.260
  122.0 2.1 %reduce_sum.45 = bf16[128,1024]{1,0:T(8,128)(2,1)} reduce(bf16[128,2,1024]{2,1,0:T(2,128)(2,1)S(1)} %gather.28, bf16[]{:T(256)} %constant.37.clone.1), dimensions={1}, to_apply=%region_5.6 | reduce | flops 131072 | bytes 786434 | tf_op jit(solution)/shard_map/reduce_sum | solution.py:87
  124.1 2.1 %multiply_reduce_fusion = bf16[128,1024]{1,0:T(8,128)(2,1)} fusion(f32[128,2,1024]{2,1,0:T(2,128)S(1)} %reshape.260, f32[128,2]{1,0:T(8,128)S(1)} %copy.45), kind=kLoop, calls=%fused_computation.15 | loop fusion | flops 393216 | bytes 1311744 | tf_op jit(solution)/shard_map/reduce_sum | solution.py:83
  126.2 0.9 reduce-scatter.5.cloned.1.call-done
  127.1 1.6 broadcast_multiply_fusion
  128.7 66.2 %reduce-scatter.3.cloned.1.call-done = f32[1,48,1024]{2,1,0:T(8,128)} async-done(((f32[1,384,1024]{2,1,0:T(8,128)}), f32[1,48,1024]{2,1,0:T(8,128)}) %reduce-scatter.3.cloned.1.call-update) | async-done | bytes 196624 | tf_op jit(solution)/shard_map/reduce_scatter | solution.py:39
  194.9 1.6 broadcast_multiply_fusion.1
  (43 shorter events, 1.3 us)
Async XLA Ops:
  7.2 47.4 %copy-start = (bf16[1,384,1024]{2,1,0:T(8,128)(2,1)S(1)}, bf16[1,384,1024]{2,1,0:T(8,128)(2,1)}, u32[]{:S(2)}) copy-start(bf16[1,384,1024]{2,1,0:T(8,128)(2,1)} %param.13) | copy-start | bytes 2359300
  7.2 7.5 %copy-start.1 = (bf16[128,1024]{1,0:T(8,128)(2,1)S(1)}, bf16[128,1024]{1,0:T(8,128)(2,1)}, u32[]{:S(2)}) copy-start(bf16[128,1024]{1,0:T(8,128)(2,1)} %param.7) | copy-start | bytes 786436
  16.8 5.4 %copy-start.2 = (bf16[128,1024]{1,0:T(8,128)(2,1)S(1)}, bf16[128,1024]{1,0:T(8,128)(2,1)}, u32[]{:S(2)}) copy-start(bf16[128,1024]{1,0:T(8,128)(2,1)} %param.8) | copy-start | bytes 786436
  18.0 18.7 %all-to-all-start = ((bf16[4,128,1024]{2,1,0:T(8,128)(2,1)}), bf16[4,128,1024]{2,1,0:T(8,128)(2,1)S(1)}, u32[]{:S(2)}, u32[]{:S(2)}) async-start(bf16[4,128,1024]{2,1,0:T(8,128)(2,1)} %broadcast_select_fusion), calls=%async_computation | async-start | bytes 2097152 | tf_op jit(solution)/shard_map/all_to_all | solution.py:73
  36.6 17.9 %all-to-all-start.2 = ((bf16[4,128,1024]{2,1,0:T(8,128)(2,1)}), bf16[4,128,1024]{2,1,0:T(8,128)(2,1)S(1)}, u32[]{:S(2)}, u32[]{:S(2)}) async-start(bf16[4,128,1024]{2,1,0:T(8,128)(2,1)} %fusion), calls=%async_computation.2 | async-start | bytes 2097152 | tf_op jit(solution)/shard_map/all_to_all | solution.py:76
  40.1 86.9 %reduce-scatter.5.cloned.1.call-start = ((), (), s32[]{:S(2)}) async-start(), calls=%async_computation.7 | async-start | bytes 1769472 | tf_op jit(solution)/shard_map/reduce_scatter | solution.py:27
  40.2 2.9 %copy-start.3 = (bf16[1,384,1024]{2,1,0:T(8,128)(2,1)S(1)}, bf16[1,384,1024]{2,1,0:T(8,128)(2,1)}, u32[]{:S(2)}) copy-start(bf16[1,384,1024]{2,1,0:T(8,128)(2,1)} %param.12) | copy-start | bytes 2359300
  57.5 0.8 copy-start.5
  60.1 134.8 %reduce-scatter.3.cloned.1.call-start = ((), (), s32[]{:S(2)}) async-start(), calls=%async_computation.6 | async-start | bytes 1769472 | tf_op jit(solution)/shard_map/reduce_scatter | solution.py:39
  60.3 1.8 copy-start.7
  62.1 2.6 %copy-start.4 = (bf16[1,384,1024]{2,1,0:T(8,128)(2,1)S(1)}, bf16[1,384,1024]{2,1,0:T(8,128)(2,1)}, u32[]{:S(2)}) copy-start(bf16[1,384,1024]{2,1,0:T(8,128)(2,1)} %param.12) | copy-start | bytes 2359300
  75.4 8.3 %copy-start.6 = (bf16[512,384]{1,0:T(8,128)(2,1)S(1)}, bf16[512,384]{1,0:T(8,128)(2,1)}, u32[]{:S(2)}) copy-start(bf16[512,384]{1,0:T(8,128)(2,1)} %copy-done.5) | copy-start | bytes 1179652
  79.2 18.8 %all-to-all-start.3 = ((bf16[4,2,65536]{2,1,0:T(2,128)(2,1)}), bf16[4,2,65536]{2,1,0:T(2,128)(2,1)}, u32[]{:S(2)}, u32[]{:S(2)}) async-start(bf16[4,2,65536]{2,1,0:T(2,128)(2,1)} %reshape.318), calls=%async_computation.3 | async-start | bytes 2097152 | tf_op jit(solution)/shard_map/all_to_all | solution.py:78
  93.8 7.9 %copy-start.8 = (s32[128,2]{0,1:T(2,128)S(1)}, s32[128,2]{0,1:T(2,128)}, u32[]{:S(2)}) copy-start(s32[128,2]{0,1:T(2,128)} %param.9) | copy-start | bytes 3076
  97.9 17.9 %all-to-all-start.1 = ((bf16[4,2,65536]{2,1,0:T(2,128)(2,1)}), bf16[4,2,65536]{2,1,0:T(2,128)(2,1)S(1)}, u32[]{:S(2)}, u32[]{:S(2)}) async-start(bf16[4,2,65536]{2,1,0:T(2,128)(2,1)} %reshape.316), calls=%async_computation.1 | async-start | bytes 2097152 | tf_op jit(solution)/shard_map/all_to_all | solution.py:75
Sparse Core Ops, SparseCore 0:
  60.2 66.8 reduce-scatter.4
  130.5 64.3 reduce-scatter.2
where the time goes:
time: 204 us; the launch traced here: 203 us
  waiting for transfers between devices  95 us (47%)
  local copies, waits for them, and re-layouts  35.7 us (18%)
  other arithmetic  27 us (13%)
  starting transfers between devices  16.3 us (8%)
  matrix products  15 us (7%)
  between operations  14.3 us (7%)
    reduce_scatter x1, waiting for transfers between devices, backward(): lax.psum_scatter(grad_upper, 'dp', scatter_dimension=1, tiled=True)  66.2 us
    unnamed x27, local copies, waits for them, and re-layouts  20.8 us
    unnamed x3, other arithmetic  15.7 us
    dot_general x8, matrix products, batched(): lax.dot_general(left_op, right_op, (((left_dim,), (right_dim,)), ((0,), (...  15 us
    all_to_all x1, waiting for transfers between devices, shards(): lax.all_to_all(sent_tokens, 'expert', split_axis=0, concat_axis=1, tiled=...  11.1 us
    all_to_all x1, waiting for transfers between devices, shards(): lax.all_to_all(sent_grads, 'expert', split_axis=0, concat_axis=1, tiled=T...  9.83 us
    all_to_all x1, waiting for transfers between devices, shards(): lax.all_to_all(expert_out, 'expert', split_axis=1, concat_axis=0, tiled=T...  6.51 us
    all_to_all x1, starting transfers between devices, shards(): lax.all_to_all(grad_input, 'expert', split_axis=1, concat_axis=0, tiled=T...  4.48 us
  transfers between devices with their start and end apart: 6, of which 6 were waited for; matrix products, arithmetic and copies ran while one was open for 29% of the time, Pallas kernels for 0%

commit v1 on v0

--- a/solution.py
+++ b/solution.py
@@ -2,6 +2,22 @@
 import jax.numpy as jnp
 from jax import lax
 from jax.sharding import PartitionSpec as P
+
+
+def swapped_with_each(x, axis, split, join):
+    ways, here = (lax.axis_size(axis), lax.axis_index(axis))
+    width = x.shape[split] // ways
+    dims = list(x.shape)
+    dims[split] = width
+    height = dims[join]
+    dims[join] = height * ways
+    full = jnp.zeros(dims, x.dtype)
+    for mask in range(ways):
+        part = lax.dynamic_slice_in_dim(x, (here ^ mask) * width, width, axis=split)
+        if mask:
+            part = lax.ppermute(part, axis, [(d, d ^ mask) for d in range(ways)])
+        full = lax.dynamic_update_slice_in_dim(full, part, (here ^ mask) * height, axis=join)
+    return full
 
 
 def batched(left_op, right_op, left_dim, right_dim):
@@ -70,7 +86,7 @@
         jnp.bfloat16
     )
     sent_grads = sent_grads.reshape(experts, capacity, model_width)
-    received = lax.all_to_all(sent_tokens, "expert", split_axis=0, concat_axis=1, tiled=True)
+    received = swapped_with_each(sent_tokens, "expert", 0, 1)
     saved_acts, expert_out = forward(received, w_gate, w_up, w_down)
     back_out = lax.all_to_all(expert_out, "expert", split_axis=1, concat_axis=0, tiled=True)
     grad_out = lax.all_to_all(sent_grads, "expert", split_axis=0, concat_axis=1, tiled=True)

time: 204 us -> 194 us (0.951)
  waiting for transfers between devices: 95 us -> 81.6 us
  local copies, waits for them, and re-layouts: 35.7 us -> 40 us
    reduce_scatter x1, waiting for transfers between devices: 0.94 us -> 66.2 us  [backward(): lax.psum_scatter(batched(hidden, grad_out, 1, 1), 'dp', scatter_dimension...]
    reduce_scatter x1, waiting for transfers between devices: 66.2 us -> 2.13 us  [backward(): lax.psum_scatter(grad_upper, 'dp', scatter_dimension=1, tiled=True)]
    all_to_all x1 -> x0, waiting for transfers between devices: 11.1 us -> none  [shards(): lax.all_to_all(sent_tokens, 'expert', split_axis=0, concat_axis=1, tiled=...]
    all_to_all x1 -> x0, starting transfers between devices: 4.24 us -> none  [shards(): lax.all_to_all(sent_tokens, 'expert', split_axis=0, concat_axis=1, tiled=...]
    dynamic_update_slice x0 -> x4, local copies, waits for them, and re-layouts: none -> 3.96 us  [swapped_with_each(): lax.dynamic_update_slice_in_dim(full, part, (here ^ mask) * height, axis=...]
    all_to_all x1, waiting for transfers between devices: 9.83 us -> 5.91 us  [shards(): lax.all_to_all(sent_grads, 'expert', split_axis=0, concat_axis=1, tiled=T...]
    ppermute x0 -> x3, starting transfers between devices: none -> 3.08 us  [swapped_with_each(): part = lax.ppermute(part, axis, [(d, d ^ mask) for d in range(ways)])]
    ppermute x0 -> x3, waiting for transfers between devices: none -> 2.55 us  [swapped_with_each(): part = lax.ppermute(part, axis, [(d, d ^ mask) for d in range(ways)])]
  transfers between devices with their start and end apart: 6 -> 8, of which waited for: 6 -> 6; matrix products, arithmetic and copies ran while one was open for 29% -> 34% of each run, Pallas kernels for 0% -> 0%
where the time goes in v1:
time: 194 us; the launch traced here: 193 us
  waiting for transfers between devices  81.6 us (42%)
  local copies, waits for them, and re-layouts  40 us (21%)
  other arithmetic  26 us (13%)
  matrix products  16.1 us (8%)
  starting transfers between devices  15.1 us (8%)
  between operations  14.4 us (7%)
    reduce_scatter x1, waiting for transfers between devices, backward(): lax.psum_scatter(batched(hidden, grad_out, 1, 1), 'dp', scatter_dimension...  66.2 us
    unnamed x27, local copies, waits for them, and re-layouts  20 us
    dot_general x8, matrix products, batched(): lax.dot_general(left_op, right_op, (((left_dim,), (right_dim,)), ((0,), (...  16.1 us
    unnamed x3, other arithmetic  15.7 us
    all_to_all x1, waiting for transfers between devices, shards(): lax.all_to_all(sent_grads, 'expert', split_axis=0, concat_axis=1, tiled=T...  5.91 us
    all_to_all x1, starting transfers between devices, shards(): lax.all_to_all(grad_input, 'expert', split_axis=1, concat_axis=0, tiled=T...  4.48 us
    all_to_all x1, waiting for transfers between devices, shards(): lax.all_to_all(expert_out, 'expert', split_axis=1, concat_axis=0, tiled=T...  4.42 us
    dynamic_update_slice x4, local copies, waits for them, and re-layouts, swapped_with_each(): lax.dynamic_update_slice_in_dim(full, part, (here ^ mask) * height, axis=...  3.96 us
  transfers between devices with their start and end apart: 8, of which 6 were waited for; matrix products, arithmetic and copies ran while one was open for 34% of the time, Pallas kernels for 0%

profile of v1, /device:TPU:0, one launch (start us, length us, event | category | flops | bytes accessed | tf_op | source)
XLA Modules:
  0.0 193.3 jit_solution(18035983641127385782)
XLA Ops:
  7.2 0.9 copy.39
  8.4 1.2 reduce-window.6
  10.2 0.8 copy.45
  11.1 3.5 %gather_fusion.2 = f32[512]{0:T(512)S(1)} fusion(f32[256]{0:T(256)S(1)} %reshape.268, s32[1024]{0:T(1024)S(1)} %pad_clamp_fusion), kind=kCustom, calls=%fused_computation.2 | custom fusion | bytes 6144 | tf_op jit(solution)/shard_map/gather | solution.py:82
  14.7 2.1 %gather_fusion = bf16[512,1024]{1,0:T(8,128)(2,1)S(1)} fusion(bf16[128,1024]{1,0:T(8,128)(2,1)S(1)} %copy-done.1, s32[1024]{0:T(1024)S(1)} %pad_clamp_fusion.2), kind=kCustom, calls=%fused_computation | custom fusion | bytes 2099200 | tf_op jit(solution)/shard_map/gather | solution.py:83
  17.0 1.0 constant_dynamic-slice_fusion
  17.9 0.5 collective-permute-start
  18.4 2.5 %collective-permute-start.1 = (bf16[1,128,1024]{2,1,0:T(8,128)(2,1)}, bf16[1,128,1024]{2,1,0:T(8,128)(2,1)}, u32[]{:S(2)}, u32[]{:S(2)}) collective-permute-start(bf16[1,128,1024]{2,1,0:T(8,128)(2,1)} %get-tuple-element.7), channel_id=1, source_target_pairs={{0,2},{1,3},{2,0},{3,1},{4,6},{5,7},{6,4},{7,5},{8,10},{9,11},{10,... | collective-permute-start | bytes 786440 | tf_op jit(solution)/shard_map/ppermute | solution.py:18
  21.0 2.0 %gather_fusion.3 = bf16[512,1024]{1,0:T(8,128)(2,1)S(1)} fusion(bf16[128,1024]{1,0:T(8,128)(2,1)S(1)} %copy-done.2, s32[1024]{0:T(1024)S(1)} %pad_clamp_fusion.2), kind=kCustom, calls=%fused_computation.3 | custom fusion | bytes 2099200 | tf_op jit(solution)/shard_map/gather | solution.py:85
  23.1 1.2 fusion
  24.3 3.5 %all-to-all-start.1 = ((bf16[4,128,1024]{2,1,0:T(8,128)(2,1)}), bf16[4,128,1024]{2,1,0:T(8,128)(2,1)S(1)}, u32[]{:S(2)}, u32[]{:S(2)}) async-start(bf16[4,128,1024]{2,1,0:T(8,128)(2,1)} %fusion), calls=%async_computation.1 | async-start | bytes 2097152 | tf_op jit(solution)/shard_map/all_to_all | solution.py:92
  28.0 1.0 bitcast_dynamic-update-slice_fusion.3
  29.1 1.0 bitcast_dynamic-update-slice_fusion.2
  30.1 1.0 bitcast_dynamic-update-slice_fusion.1
  31.1 2.5 %collective-permute-done.2 = bf16[1,128,1024]{2,1,0:T(8,128)(2,1)} collective-permute-done((bf16[1,128,1024]{2,1,0:T(8,128)(2,1)S(1)}, bf16[1,128,1024]{2,1,0:T(8,128)(2,1)}, u32[]{:S(2)}, u32[]{:S(2)}) %collective-permute-start.2) | collective-permute-done | bytes 262176 | tf_op jit(solution)/shard_map/ppermute | solution.py:18
  33.6 1.0 bitcast_dynamic-update-slice_fusion
  34.6 2.8 %fusion.11 = f32[512,384]{1,0:T(8,128)} fusion(bf16[512,1024]{1,0:T(8,128)(2,1)S(1)} %bitcast_dynamic-update-slice_fusion, bf16[1,384,1024]{2,1,0:T(8,128)(2,1)} %param.11), kind=kOutput, calls=%fused_computation.25 | convolution fusion | flops 402653184 | bytes 2621440 | tf_op jit(solution)/shard_map/dot_general | solution.py:24
  37.4 1.6 fusion.7
  39.0 5.9 %all-to-all-done.1 = bf16[4,128,1024]{2,1,0:T(8,128)(2,1)S(1)} async-done(((bf16[4,128,1024]{2,1,0:T(8,128)(2,1)}), bf16[4,128,1024]{2,1,0:T(8,128)(2,1)S(1)}, u32[]{:S(2)}, u32[]{:S(2)}) %all-to-all-start.1) | async-done | bytes 1048608 | tf_op jit(solution)/shard_map/all_to_all | solution.py:92
  45.0 3.1 %multiply_convert_fusion = (bf16[512,384]{1,0:T(8,128)(2,1)S(1)}, bf16[512,384]{1,0:T(8,128)(2,1)}, f32[512,384]{1,0:T(8,128)}) fusion(f32[512,384]{1,0:T(8,128)} %fusion.11, f32[512,384]{1,0:T(8,128)} %fusion.7, bf16[512,1024]{1,0:T(8,128)(2,1)S(1)} %bitcast.96, bf16[1,384,1024]{2,1,0:T(8,128)(2,1)S(1)} %copy-done), kind=kOutput, calls=%fused_computation.27 | convolution fusion | flops 404422656 | bytes 4980736 | tf_op jit(solution)/shard_map/dot_general | solution.py:24
  48.1 1.7 convolution_bitcast_fusion.1
  50.1 2.8 %convolution_bitcast_fusion = f32[1,384,1024]{2,1,0:T(8,128)} fusion(bf16[512,384]{1,0:T(8,128)(2,1)} %get-tuple-element.10, bf16[512,1024]{1,0:T(8,128)(2,1)S(1)} %bitcast.97), kind=kOutput, calls=%fused_computation.8 | convolution fusion | flops 402653184 | bytes 3014656 | tf_op jit(solution)/shard_map/dot_general | solution.py:24
  53.0 2.6 %fusion.9 = f32[512,1024]{1,0:T(8,128)S(1)} fusion(bf16[1,384,1024]{2,1,0:T(8,128)(2,1)S(1)} %copy-done.7, f32[512,384]{1,0:T(8,128)} %fusion.11, f32[512,384]{1,0:T(8,128)} %get-tuple-element.13, f32[512,384]{1,0:T(8,128)} %fusion.7), kind=kOutput, calls=%fused_computation.23 | convolution fusion | flops 404619264 | bytes 5242880 | tf_op jit(solution)/shard_map/dot_general | solution.py:24
  55.6 0.7 fusion.2
  56.3 1.6 copy.58
  57.9 0.5 broadcast.260
  58.4 7.8 %reduce.2 = bf16[512,1024]{1,0:T(8,128)(2,1)} reduce(bf16[512,1,1024]{2,1,0:T(2,128)(2,1)S(1)} %bitcast.92, bf16[]{:T(256)} %broadcast.260), dimensions={1}, to_apply=%bitcast.86.reduce_sub_computation | reduce | bytes 2097154
  66.2 3.8 %reshape.329 = bf16[4,2,65536]{2,1,0:T(2,128)(2,1)} reshape(bf16[512,1024]{1,0:T(8,128)(2,1)} %reduce.2) | data formatting | bytes 2097152
  70.0 4.5 %all-to-all-start.2 = ((bf16[4,2,65536]{2,1,0:T(2,128)(2,1)}), bf16[4,2,65536]{2,1,0:T(2,128)(2,1)}, u32[]{:S(2)}, u32[]{:S(2)}) async-start(bf16[4,2,65536]{2,1,0:T(2,128)(2,1)} %reshape.329), calls=%async_computation.2 | async-start | bytes 2097152 | tf_op jit(solution)/shard_map/all_to_all | solution.py:94
  74.5 0.7 fusion.1
  75.2 1.6 copy.59
  76.8 7.8 %reduce.1 = bf16[512,1024]{1,0:T(8,128)(2,1)} reduce(bf16[512,1,1024]{2,1,0:T(2,128)(2,1)S(1)} %bitcast.93, bf16[]{:T(256)} %broadcast.260), dimensions={1}, to_apply=%bitcast.87.reduce_sub_computation | reduce | bytes 2097154
  84.7 3.7 %reshape.327 = bf16[4,2,65536]{2,1,0:T(2,128)(2,1)} reshape(bf16[512,1024]{1,0:T(8,128)(2,1)} %reduce.1) | data formatting | bytes 2097152
  88.8 3.8 %all-to-all-start = ((bf16[4,2,65536]{2,1,0:T(2,128)(2,1)}), bf16[4,2,65536]{2,1,0:T(2,128)(2,1)S(1)}, u32[]{:S(2)}, u32[]{:S(2)}) async-start(bf16[4,2,65536]{2,1,0:T(2,128)(2,1)} %reshape.327), calls=%async_computation | async-start | bytes 2097152 | tf_op jit(solution)/shard_map/all_to_all | solution.py:91
  92.9 4.0 %reshape.330 = bf16[512,1,1024]{2,1,0:T(2,128)(2,1)} reshape(bf16[4,2,65536]{2,1,0:T(2,128)(2,1)} %all-to-all-done.2) | data formatting | bytes 2097152
  96.8 2.0 %copy.56 = bf16[1,512,1024]{2,1,0:T(8,128)(2,1)S(1)} copy(bf16[1,512,1024]{2,0,1:T(2,128)(2,1)} %bitcast.90) | data formatting | bytes 2097152
  98.8 1.2 gather_fusion.4
  100.2 2.1 %reduce_sum.45 = bf16[128,1024]{1,0:T(8,128)(2,1)} reduce(bf16[128,2,1024]{2,1,0:T(2,128)(2,1)S(1)} %gather.28, bf16[]{:T(256)} %constant.21.clone.1), dimensions={1}, to_apply=%region_5.6 | reduce | flops 131072 | bytes 786434 | tf_op jit(solution)/shard_map/reduce_sum | solution.py:103
  102.3 4.4 %all-to-all-done = bf16[4,2,65536]{2,1,0:T(2,128)(2,1)S(1)} async-done(((bf16[4,2,65536]{2,1,0:T(2,128)(2,1)}), bf16[4,2,65536]{2,1,0:T(2,128)(2,1)S(1)}, u32[]{:S(2)}, u32[]{:S(2)}) %all-to-all-start) | async-done | bytes 1048608 | tf_op jit(solution)/shard_map/all_to_all | solution.py:91
  106.7 2.3 %reshape.328 = bf16[512,1,1024]{2,1,0:T(2,128)(2,1)} reshape(bf16[4,2,65536]{2,1,0:T(2,128)(2,1)S(1)} %all-to-all-done) | data formatting | bytes 2097152
  109.0 2.0 %copy.57 = bf16[1,512,1024]{2,1,0:T(8,128)(2,1)S(1)} copy(bf16[1,512,1024]{2,0,1:T(2,128)(2,1)} %bitcast.91) | data formatting | bytes 2097152
  111.0 1.2 gather_fusion.1
  112.2 0.7 reshape.271
  112.8 2.1 %multiply_reduce_fusion = bf16[128,1024]{1,0:T(8,128)(2,1)} fusion(f32[128,2,1024]{2,1,0:T(2,128)S(1)} %reshape.271, f32[128,2]{1,0:T(8,128)S(1)} %copy.45), kind=kLoop, calls=%fused_computation.15 | loop fusion | flops 393216 | bytes 1311744 | tf_op jit(solution)/shard_map/reduce_sum | solution.py:99
  114.9 2.1 %reduce-scatter.3.cloned.1.call-done = f32[1,48,1024]{2,1,0:T(8,128)} async-done(((f32[1,384,1024]{2,1,0:T(8,128)}), f32[1,48,1024]{2,1,0:T(8,128)}) %reduce-scatter.3.cloned.1.call-update) | async-done | bytes 196624 | tf_op jit(solution)/shard_map/reduce_scatter | solution.py:55
  117.0 1.6 broadcast_multiply_fusion.1
  118.6 66.2 %reduce-scatter.5.cloned.1.call-done = f32[1,48,1024]{2,1,0:T(8,128)} async-done(((f32[1,384,1024]{2,1,0:T(8,128)}), f32[1,48,1024]{2,1,0:T(8,128)}) %reduce-scatter.5.cloned.1.call-update) | async-done | bytes 196624 | tf_op jit(solution)/shard_map/reduce_scatter | solution.py:43
  184.8 1.6 broadcast_multiply_fusion
  (53 shorter events, 2.6 us)
Async XLA Ops:
  7.2 37.8 %copy-start = (bf16[1,384,1024]{2,1,0:T(8,128)(2,1)S(1)}, bf16[1,384,1024]{2,1,0:T(8,128)(2,1)}, u32[]{:S(2)}) copy-start(bf16[1,384,1024]{2,1,0:T(8,128)(2,1)} %param.13) | copy-start | bytes 2359300
  7.2 7.5 %copy-start.1 = (bf16[128,1024]{1,0:T(8,128)(2,1)S(1)}, bf16[128,1024]{1,0:T(8,128)(2,1)}, u32[]{:S(2)}) copy-start(bf16[128,1024]{1,0:T(8,128)(2,1)} %param.7) | copy-start | bytes 786436
  16.8 4.3 %copy-start.2 = (bf16[128,1024]{1,0:T(8,128)(2,1)S(1)}, bf16[128,1024]{1,0:T(8,128)(2,1)}, u32[]{:S(2)}) copy-start(bf16[128,1024]{1,0:T(8,128)(2,1)} %param.8) | copy-start | bytes 786436
  16.9 6.2 %copy-start.3 = (bf16[4,128,1024]{2,1,0:T(8,128)(2,1)}, bf16[4,128,1024]{2,1,0:T(8,128)(2,1)S(1)}, u32[]{:S(2)}) copy-start(bf16[4,128,1024]{2,1,0:T(8,128)(2,1)S(1)} %broadcast_select_fusion) | copy-start | bytes 3145732
  17.9 11.1 %collective-permute-start = (bf16[1,128,1024]{2,1,0:T(8,128)(2,1)}, bf16[1,128,1024]{2,1,0:T(8,128)(2,1)}, u32[]{:S(2)}, u32[]{:S(2)}) collective-permute-start(bf16[1,128,1024]{2,1,0:T(8,128)(2,1)} %get-tuple-element.8), channel_id=1, source_target_pairs={{0,1},{1,0},{2,3},{3,2},{4,5},{5,4},{6,7},{7,6},{8,9},{9,8},{10,11... | collective-permute-start | bytes 786440 | tf_op jit(solution)/shard_map/ppermute | solution.py:18
  18.4 11.7 %collective-permute-start.1 = (bf16[1,128,1024]{2,1,0:T(8,128)(2,1)}, bf16[1,128,1024]{2,1,0:T(8,128)(2,1)}, u32[]{:S(2)}, u32[]{:S(2)}) collective-permute-start(bf16[1,128,1024]{2,1,0:T(8,128)(2,1)} %get-tuple-element.7), channel_id=1, source_target_pairs={{0,2},{1,3},{2,0},{3,1},{4,6},{5,7},{6,4},{7,5},{8,10},{9,11},{10,... | collective-permute-start | bytes 786440 | tf_op jit(solution)/shard_map/ppermute | solution.py:18
  20.9 12.7 %collective-permute-start.2 = (bf16[1,128,1024]{2,1,0:T(8,128)(2,1)S(1)}, bf16[1,128,1024]{2,1,0:T(8,128)(2,1)}, u32[]{:S(2)}, u32[]{:S(2)}) collective-permute-start(bf16[1,128,1024]{2,1,0:T(8,128)(2,1)S(1)} %get-tuple-element.6), channel_id=1, source_target_pairs={{0,3},{1,2},{2,1},{3,0},{4,7},{5,6},{6,5},{7,4},{8,11},{9,10},{10,... | collective-permute-start | bytes 786440 | tf_op jit(solution)/shard_map/ppermute | solution.py:18
  24.3 20.6 %all-to-all-start.1 = ((bf16[4,128,1024]{2,1,0:T(8,128)(2,1)}), bf16[4,128,1024]{2,1,0:T(8,128)(2,1)S(1)}, u32[]{:S(2)}, u32[]{:S(2)}) async-start(bf16[4,128,1024]{2,1,0:T(8,128)(2,1)} %fusion), calls=%async_computation.1 | async-start | bytes 2097152 | tf_op jit(solution)/shard_map/all_to_all | solution.py:92
  27.9 89.2 %reduce-scatter.3.cloned.1.call-start = ((), (), s32[]{:S(2)}) async-start(), calls=%async_computation.5 | async-start | bytes 1769472 | tf_op jit(solution)/shard_map/reduce_scatter | solution.py:55
  29.0 8.4 %copy-start.4 = (bf16[1,384,1024]{2,1,0:T(8,128)(2,1)S(1)}, bf16[1,384,1024]{2,1,0:T(8,128)(2,1)}, u32[]{:S(2)}) copy-start(bf16[1,384,1024]{2,1,0:T(8,128)(2,1)} %param.12) | copy-start | bytes 2359300
  49.9 134.9 %reduce-scatter.5.cloned.1.call-start = ((), (), s32[]{:S(2)}) async-start(), calls=%async_computation.6 | async-start | bytes 1769472 | tf_op jit(solution)/shard_map/reduce_scatter | solution.py:43
  50.1 2.9 %copy-start.7 = (bf16[1,384,1024]{2,1,0:T(8,128)(2,1)S(1)}, bf16[1,384,1024]{2,1,0:T(8,128)(2,1)}, u32[]{:S(2)}) copy-start(bf16[1,384,1024]{2,1,0:T(8,128)(2,1)} %param.11) | copy-start | bytes 2359300
  53.0 2.6 %copy-start.5 = (bf16[1,384,1024]{2,1,0:T(8,128)(2,1)S(1)}, bf16[1,384,1024]{2,1,0:T(8,128)(2,1)}, u32[]{:S(2)}) copy-start(bf16[1,384,1024]{2,1,0:T(8,128)(2,1)} %param.12) | copy-start | bytes 2359300
  66.2 8.3 %copy-start.6 = (bf16[512,384]{1,0:T(8,128)(2,1)S(1)}, bf16[512,384]{1,0:T(8,128)(2,1)}, u32[]{:S(2)}) copy-start(bf16[512,384]{1,0:T(8,128)(2,1)} %get-tuple-element.10) | copy-start | bytes 1179652
  70.0 18.8 %all-to-all-start.2 = ((bf16[4,2,65536]{2,1,0:T(2,128)(2,1)}), bf16[4,2,65536]{2,1,0:T(2,128)(2,1)}, u32[]{:S(2)}, u32[]{:S(2)}) async-start(bf16[4,2,65536]{2,1,0:T(2,128)(2,1)} %reshape.329), calls=%async_computation.2 | async-start | bytes 2097152 | tf_op jit(solution)/shard_map/all_to_all | solution.py:94
  84.7 7.9 %copy-start.8 = (s32[128,2]{0,1:T(2,128)S(1)}, s32[128,2]{0,1:T(2,128)}, u32[]{:S(2)}) copy-start(s32[128,2]{0,1:T(2,128)} %param.9) | copy-start | bytes 3076
  88.8 17.9 %all-to-all-start = ((bf16[4,2,65536]{2,1,0:T(2,128)(2,1)}), bf16[4,2,65536]{2,1,0:T(2,128)(2,1)S(1)}, u32[]{:S(2)}, u32[]{:S(2)}) async-start(bf16[4,2,65536]{2,1,0:T(2,128)(2,1)} %reshape.327), calls=%async_computation | async-start | bytes 2097152 | tf_op jit(solution)/shard_map/all_to_all | solution.py:91
Sparse Core Ops, SparseCore 0:
  50.0 67.0 reduce-scatter.2
  120.4 64.3 reduce-scatter.4
